TPU v7x, 32 devices: a whole 2x2x4 slice. The times are simulated.
32 devices in a mesh: section: 2 (over x), gy: 4 (over y, core), gx: 4 (over z).
Axes of the slice: x: 2, y: 2, z: 4, core: 2. Of those that a mesh axis runs over, the one named last changes fastest.
Arguments:
- images: bfloat16 [2, 128, 256, 128], P('section', 'gy', 'gx'), may hold values from -6 to 6
- first_kernel: bfloat16 [3, 3, 128, 128], replicated, may hold values from -0.1875 to 0.1875
- projection: bfloat16 [128, 256], replicated, may hold values from -0.5 to 0.5
- second_kernel: bfloat16 [3, 3, 256, 256], replicated, may hold values from -0.125 to 0.125
- cotangent: bfloat16 [2, 64, 128, 256], P('section', 'gy', 'gx'), may hold values from -0.625 to 0.625
Outputs:
- features: bfloat16 [2, 64, 128, 256], P('section', 'gy', 'gx')
- grad_first: float32 [3, 3, 128, 128], replicated
- grad_projection: float32 [128, 256], replicated
- grad_second: float32 [3, 3, 256, 256], replicated
All inputs are finite; a program needn't handle non-finite values.
Results may differ from a plain program's by a relative error of at most 0.014.
Values may be sent and summed in bfloat16 or wider, within the bound.
No kernel may reach another device: no remote copies, remote signals or barrier semaphores. Data moves between devices by JAX's collectives and lax.ppermute only.
A program may use at most 64 MiB of HBM per device.

v0:
```python
import jax
import jax.numpy as jnp
from jax import lax
from jax.sharding import PartitionSpec as P


def padded_2(array, sides, width):
    for axis, dim in sides:
        size, length = (lax.axis_size(axis), array.shape[dim])
        up = [(i, (i + 1) % size) for i in range(size - 1)]
        down = [(j, i) for i, j in up]
        last = lax.slice_in_dim(array, length - width, length, axis=dim)
        initial = lax.slice_in_dim(array, 0, width, axis=dim)
        before = lax.ppermute(last, axis, up)
        after = lax.ppermute(initial, axis, down)
        array = jnp.concatenate([before, array, after], axis=dim)
    return array


def from_partner(block, axis, bit):
    count = lax.axis_size(axis)
    route = []
    for low in range(count):
        high = low | 1 << bit
        if high != low and high < count:
            route += [(low, high), (high, low)]
    return lax.ppermute(block, axis, route)


def silu_slope(values):
    sigma = jax.nn.sigmoid(values)
    return sigma * (1.0 + values * (1.0 - sigma))


def conv_forward(padded, kernel, row_count, col_count):
    total = jnp.zeros((row_count * col_count, kernel.shape[3]), jnp.float32)
    for row_tap in range(3):
        for col_tap in range(3):
            piece = padded[row_tap : row_tap + row_count, col_tap : col_tap + col_count].reshape(
                row_count * col_count, padded.shape[2]
            )
            total = total + jnp.dot(
                piece, kernel[row_tap, col_tap], preferred_element_type=jnp.float32
            )
    return total


def conv_slopes(padded, slope, row_count, col_count):
    pieces = []
    for row_tap in range(3):
        for col_tap in range(3):
            piece = padded[row_tap : row_tap + row_count, col_tap : col_tap + col_count].reshape(
                row_count * col_count, padded.shape[2]
            )
            pieces.append(jnp.einsum("pc,pd->cd", piece, slope, preferred_element_type=jnp.float32))
    return jnp.stack(pieces).reshape(3, 3, padded.shape[2], slope.shape[1])


def conv_back(padded, kernel, row_count, col_count):
    total = jnp.zeros((row_count * col_count, kernel.shape[2]), jnp.float32)
    for row_tap in range(3):
        for col_tap in range(3):
            piece = padded[
                2 - row_tap : 2 - row_tap + row_count, 2 - col_tap : 2 - col_tap + col_count
            ].reshape(row_count * col_count, padded.shape[2])
            total = total + jnp.einsum(
                "pd,cd->pc", piece, kernel[row_tap, col_tap], preferred_element_type=jnp.float32
            )
    return total


def first_forward(tile, first_kernel):
    row_count, col_count, channels = tile.shape
    padded = padded_2(tile, (("gy", 0), ("gx", 1)), 1)
    before = conv_forward(padded, first_kernel, row_count, col_count)
    hidden = jax.nn.silu(before).astype(jnp.bfloat16).reshape(row_count, col_count, channels)
    pooled = (
        hidden.astype(jnp.float32)
        .reshape(row_count // 2, 2, col_count // 2, 2, channels)
        .sum(axis=(1, 3))
        * 0.25
    ).astype(jnp.bfloat16)
    return (padded, before, pooled)


def project(pooled, projection):
    half_rows, half_cols, channels = pooled.shape
    flat = jnp.dot(
        pooled.reshape(half_rows * half_cols, channels),
        projection,
        preferred_element_type=jnp.float32,
    )
    return flat.astype(jnp.bfloat16).reshape(half_rows, half_cols, projection.shape[1])


def second_pass(middle, second_kernel, upstream):
    half_rows, half_cols, wide = middle.shape
    padded = padded_2(middle, (("gy", 0), ("gx", 1)), 1)
    before = conv_forward(padded, second_kernel, half_rows, half_cols)
    output = jax.nn.silu(before).astype(jnp.bfloat16).reshape(half_rows, half_cols, wide)
    flat_up = upstream.reshape(half_rows * half_cols, wide).astype(jnp.float32)
    slope = (flat_up * silu_slope(before)).astype(jnp.bfloat16)
    kernel_grad = conv_slopes(padded, slope, half_rows, half_cols)
    slope_padded = padded_2(slope.reshape(half_rows, half_cols, wide), (("gy", 0), ("gx", 1)), 1)
    back = conv_back(slope_padded, second_kernel, half_rows, half_cols).astype(jnp.bfloat16)
    return (output, kernel_grad, back.reshape(half_rows, half_cols, wide))


def projection_back(pooled, back, projection):
    half_rows, half_cols, channels = pooled.shape
    flat_pool = pooled.reshape(half_rows * half_cols, channels)
    flat_back = back.reshape(half_rows * half_cols, back.shape[2])
    grad = jnp.einsum("pc,pd->cd", flat_pool, flat_back, preferred_element_type=jnp.float32)
    pooled_slope = jnp.einsum(
        "pd,cd->pc", flat_back, projection, preferred_element_type=jnp.float32
    )
    return (grad, pooled_slope.astype(jnp.bfloat16).reshape(half_rows, half_cols, channels))


def first_back(padded, before, pooled_slope):
    half_rows, half_cols, channels = pooled_slope.shape
    spread = jnp.broadcast_to(
        (pooled_slope.astype(jnp.float32) * 0.25)[:, None, :, None, :],
        (half_rows, 2, half_cols, 2, channels),
    )
    spread = spread.reshape(4 * half_rows * half_cols, channels)
    slope = (spread * silu_slope(before)).astype(jnp.bfloat16)
    return conv_slopes(padded, slope, 2 * half_rows, 2 * half_cols)


def per_device(images, first_kernel, projection, second_kernel, cotangent):
    padded, before, pooled = first_forward(images[0], first_kernel)
    upstream = from_partner(cotangent[0], "section", 0)
    middle = project(pooled, projection)
    output, grad_second, back = second_pass(middle, second_kernel, upstream)
    grad_projection, pooled_slope = projection_back(pooled, back, projection)
    output = from_partner(output, "section", 0)
    grad_first = first_back(padded, before, pooled_slope)
    grad_first, grad_projection, grad_second = lax.psum(
        (grad_first, grad_projection, grad_second), ("section", "gy", "gx")
    )
    return (output[None], grad_first, grad_projection, grad_second)


def solution(mesh):
    placed = (P("section", "gy", "gx", None), P(), P(), P(), P("section", "gy", "gx", None))
    return jax.shard_map(
        per_device,
        mesh=mesh,
        in_specs=placed,
        out_specs=(P("section", "gy", "gx", None), P(), P(), P()),
        check_vma=False,
    )
```

profile of v0, /device:TPU:0, one launch (start us, length us, event | category | flops | bytes accessed | tf_op | source)
XLA Modules:
  0.0 227.4 jit_solution(3787896188777336523)
XLA Ops:
  7.2 0.8 slice_bitcast_fusion.5
  8.0 2.4 %collective-permute-start = (bf16[1,64,128]{2,1,0:T(8,128)(2,1)S(1)}, bf16[1,64,128]{2,1,0:T(8,128)(2,1)S(1)}, u32[]{:S(2)}, u32[]{:S(2)}) collective-permute-start(bf16[1,64,128]{2,1,0:T(8,128)(2,1)S(1)} %get-tuple-element.21), channel_id=1, source_target_pairs={{0,4},{4,8},{8,12},{1,5},{5,9},{9,13},{2,6},{6,10},{10,14},{3,7},{... | collective-permute-start | bytes 49160 | tf_op jit(solution)/shard_map/ppermute | solution.py:14
  10.4 1.3 collective-permute-start.1
  11.7 3.9 %collective-permute-done.1 = bf16[1,64,128]{2,1,0:T(8,128)(2,1)S(1)} collective-permute-done((bf16[1,64,128]{2,1,0:T(8,128)(2,1)S(1)}, bf16[1,64,128]{2,1,0:T(8,128)(2,1)S(1)}, u32[]{:S(2)}, u32[]{:S(2)}) %collective-permute-start.1) | collective-permute-done | bytes 16416 | tf_op jit(solution)/shard_map/ppermute | solution.py:15
  15.6 0.9 pad_maximum_fusion.17
  16.5 3.5 %collective-permute-start.2 = (bf16[34,1,128]{2,1,0:T(2,128)(2,1)S(1)}, bf16[34,1,128]{2,1,0:T(2,128)(2,1)S(1)}, u32[]{:S(2)}, u32[]{:S(2)}) collective-permute-start(bf16[34,1,128]{2,1,0:T(2,128)(2,1)S(1)} %get-tuple-element.15), channel_id=1, source_target_pairs={{0,1},{1,2},{2,3},{4,5},{5,6},{6,7},{8,9},{9,10},{10,11},{12,13},{... | collective-permute-start | bytes 26120 | tf_op jit(solution)/shard_map/ppermute | solution.py:14
  20.0 1.4 collective-permute-start.3
  21.5 1.3 pad_maximum_fusion.1
  23.1 2.8 %collective-permute-done.3 = bf16[34,1,128]{2,1,0:T(2,128)(2,1)S(1)} collective-permute-done((bf16[34,1,128]{2,1,0:T(2,128)(2,1)S(1)}, bf16[34,1,128]{2,1,0:T(2,128)(2,1)S(1)}, u32[]{:S(2)}, u32[]{:S(2)}) %collective-permute-start.3) | collective-permute-done | bytes 8736 | tf_op jit(solution)/shard_map/ppermute | solution.py:15
  25.8 0.3 maximum_maximum_fusion
  26.2 0.6 fusion.85
  26.8 0.3 fusion.65
  28.8 0.5 multiply_convert_fusion.1
  29.3 0.9 convert_reduce_fusion
  30.4 3.0 %collective-permute-start.4 = (bf16[1,32,256]{2,1,0:T(8,128)(2,1)S(1)}, bf16[1,32,256]{2,1,0:T(8,128)(2,1)S(1)}, u32[]{:S(2)}, u32[]{:S(2)}) collective-permute-start(bf16[1,32,256]{2,1,0:T(8,128)(2,1)S(1)} %get-tuple-element.49), channel_id=1, source_target_pairs={{0,4},{4,8},{8,12},{1,5},{5,9},{9,13},{2,6},{6,10},{10,14},{3,7},{... | collective-permute-start | bytes 49160 | tf_op jit(solution)/shard_map/ppermute | solution.py:14
  33.4 1.3 collective-permute-start.5
  34.7 1.6 collective-permute-start.9
  36.3 1.2 collective-permute-done.5
  37.5 3.5 %collective-permute-start.6 = (bf16[18,1,256]{2,1,0:T(2,128)(2,1)S(1)}, bf16[18,1,256]{2,1,0:T(2,128)(2,1)S(1)}, u32[]{:S(2)}, u32[]{:S(2)}) collective-permute-start(bf16[18,1,256]{2,1,0:T(2,128)(2,1)S(1)} %get-tuple-element.41), channel_id=1, source_target_pairs={{0,1},{1,2},{2,3},{4,5},{5,6},{6,7},{8,9},{9,10},{10,11},{12,13},{... | collective-permute-start | bytes 27656 | tf_op jit(solution)/shard_map/ppermute | solution.py:14
  40.9 1.3 collective-permute-start.7
  42.5 4.1 %collective-permute-done.7 = bf16[18,1,256]{2,1,0:T(2,128)(2,1)S(1)} collective-permute-done((bf16[18,1,256]{2,1,0:T(2,128)(2,1)S(1)}, bf16[18,1,256]{2,1,0:T(2,128)(2,1)S(1)}, u32[]{:S(2)}, u32[]{:S(2)}) %collective-permute-start.7) | collective-permute-done | bytes 9248 | tf_op jit(solution)/shard_map/ppermute | solution.py:15
  48.7 0.4 fusion.24
  49.4 3.2 %collective-permute-start.10 = (bf16[1,32,256]{2,1,0:T(8,128)(2,1)S(1)}, bf16[1,32,256]{2,1,0:T(8,128)(2,1)S(1)}, u32[]{:S(2)}, u32[]{:S(2)}) collective-permute-start(bf16[1,32,256]{2,1,0:T(8,128)(2,1)S(1)} %get-tuple-element.45), channel_id=1, source_target_pairs={{0,4},{4,8},{8,12},{1,5},{5,9},{9,13},{2,6},{6,10},{10,14},{3,7},{... | collective-permute-start | bytes 49160 | tf_op jit(solution)/shard_map/ppermute | solution.py:14
  52.6 1.3 collective-permute-start.11
  56.2 0.3 collective-permute-done.11
  56.5 1.3 collective-permute-start.12
  57.8 4.7 %collective-permute-start.13 = (bf16[18,1,256]{2,1,0:T(2,128)(2,1)S(1)}, bf16[18,1,256]{2,1,0:T(2,128)(2,1)S(1)}, u32[]{:S(2)}, u32[]{:S(2)}) collective-permute-start(bf16[18,1,256]{2,1,0:T(2,128)(2,1)S(1)} %get-tuple-element.38), channel_id=1, source_target_pairs={{0,1},{1,2},{2,3},{4,5},{5,6},{6,7},{8,9},{9,10},{10,11},{12,13},{... | collective-permute-start | bytes 27656 | tf_op jit(solution)/shard_map/ppermute | solution.py:14
  62.9 0.9 collective-permute-done.13
  66.4 0.9 fusion.91
  67.5 0.5 broadcast_in_dim.10
  68.0 0.4 multiply_convert_fusion
  68.4 0.3 fusion.23
  68.8 0.4 fusion.22
  69.1 0.4 fusion.21
  69.5 0.4 fusion.20
  69.8 0.4 fusion.19
  70.2 0.4 fusion.18
  70.5 0.4 fusion.17
  70.9 0.4 fusion.16
  71.3 0.4 fusion.15
  71.6 0.8 copy-done.4
  72.5 1.4 collective-permute-start.8
  73.9 7.5 %collective-permute-done.8 = bf16[16,32,256]{2,1,0:T(8,128)(2,1)S(1)} collective-permute-done((bf16[16,32,256]{2,1,0:T(8,128)(2,1)S(1)}, bf16[16,32,256]{2,1,0:T(8,128)(2,1)S(1)}, u32[]{:S(2)}, u32[]{:S(2)}) %collective-permute-start.8) | collective-permute-done | bytes 262176 | tf_op jit(solution)/shard_map/ppermute | solution.py:27
  81.3 132.7 %all-reduce.3.cloned.1.call-done = (f32[3,3,128,128]{3,2,1,0:T(8,128)}, f32[128,256]{1,0:T(8,128)}, f32[3,3,256,256]{3,2,1,0:T(8,128)}) async-done(((f32[3,3,128,128]{3,2,1,0:T(8,128)}, f32[128,256]{1,0:T(8,128)}, f32[3,3,256,256]{3,2,1,0:T(8,128)}), (f32[3,3,128,128]{3,2,1,0:T(8,128)}, f32[128,256]{1,0:T(8,128)}, f32[3,3,256,256]{3,2,1,0:T(8,128)})) %all-reduce.3.cloned.1.call-update) | async-done | bytes 3080208 | tf_op jit(solution)/shard_map/psum | solution.py:139
  214.0 0.7 copy.31
  214.8 1.9 copy.32
  216.7 0.7 copy.33
  217.3 3.2 %copy.34 = f32[3,3,256,256]{3,2,1,0:T(8,128)} copy(f32[3,3,256,256]{3,2,1,0:T(8,128)} %get-tuple-element.63) | data formatting | bytes 4718592
  (72 shorter events, 10.0 us)
Async XLA Ops:
  7.2 23.0 %copy-start = (bf16[128,256]{1,0:T(8,128)(2,1)S(1)}, bf16[128,256]{1,0:T(8,128)(2,1)}, u32[]{:S(2)}) copy-start(bf16[128,256]{1,0:T(8,128)(2,1)} %param.7) | copy-start | bytes 196612
  7.2 15.6 %copy-start.5 = (bf16[3,3,128,128]{3,2,1,0:T(8,128)(2,1)S(1)}, bf16[3,3,128,128]{3,2,1,0:T(8,128)(2,1)}, u32[]{:S(2)}) copy-start(bf16[3,3,128,128]{3,2,1,0:T(8,128)(2,1)} %param.6) | copy-start | bytes 884740
  7.2 206.9 %all-reduce.3.cloned.1.call-start = ((), (), s32[]{:S(2)}) async-start(), calls=%async_computation | async-start | bytes 6160384 | tf_op jit(solution)/shard_map/psum | solution.py:139
  8.0 3.7 %collective-permute-start = (bf16[1,64,128]{2,1,0:T(8,128)(2,1)S(1)}, bf16[1,64,128]{2,1,0:T(8,128)(2,1)S(1)}, u32[]{:S(2)}, u32[]{:S(2)}) collective-permute-start(bf16[1,64,128]{2,1,0:T(8,128)(2,1)S(1)} %get-tuple-element.21), channel_id=1, source_target_pairs={{0,4},{4,8},{8,12},{1,5},{5,9},{9,13},{2,6},{6,10},{10,14},{3,7},{... | collective-permute-start | bytes 49160 | tf_op jit(solution)/shard_map/ppermute | solution.py:14
  10.4 5.2 %collective-permute-start.1 = (bf16[1,64,128]{2,1,0:T(8,128)(2,1)S(1)}, bf16[1,64,128]{2,1,0:T(8,128)(2,1)S(1)}, u32[]{:S(2)}, u32[]{:S(2)}) collective-permute-start(bf16[1,64,128]{2,1,0:T(8,128)(2,1)S(1)} %get-tuple-element.22), channel_id=1, source_target_pairs={{4,0},{8,4},{12,8},{5,1},{9,5},{13,9},{6,2},{10,6},{14,10},{7,3},{... | collective-permute-start | bytes 49160 | tf_op jit(solution)/shard_map/ppermute | solution.py:15
  16.5 6.5 %collective-permute-start.2 = (bf16[34,1,128]{2,1,0:T(2,128)(2,1)S(1)}, bf16[34,1,128]{2,1,0:T(2,128)(2,1)S(1)}, u32[]{:S(2)}, u32[]{:S(2)}) collective-permute-start(bf16[34,1,128]{2,1,0:T(2,128)(2,1)S(1)} %get-tuple-element.15), channel_id=1, source_target_pairs={{0,1},{1,2},{2,3},{4,5},{5,6},{6,7},{8,9},{9,10},{10,11},{12,13},{... | collective-permute-start | bytes 26120 | tf_op jit(solution)/shard_map/ppermute | solution.py:14
  20.0 5.8 %copy-start.1 = (bf16[1,32,64,128]{3,2,1,0:T(8,128)(2,1)S(1)}, bf16[1,32,64,128]{3,2,1,0:T(8,128)(2,1)}, u32[]{:S(2)}) copy-start(bf16[1,32,64,128]{3,2,1,0:T(8,128)(2,1)} %param.5) | copy-start | bytes 1572868
  20.0 5.8 %collective-permute-start.3 = (bf16[34,1,128]{2,1,0:T(2,128)(2,1)S(1)}, bf16[34,1,128]{2,1,0:T(2,128)(2,1)S(1)}, u32[]{:S(2)}, u32[]{:S(2)}) collective-permute-start(bf16[34,1,128]{2,1,0:T(2,128)(2,1)S(1)} %get-tuple-element.16), channel_id=1, source_target_pairs={{1,0},{2,1},{3,2},{5,4},{6,5},{7,6},{9,8},{10,9},{11,10},{13,12},{... | collective-permute-start | bytes 26120 | tf_op jit(solution)/shard_map/ppermute | solution.py:15
  29.2 5.4 %copy-start.7 = (bf16[1,16,32,256]{3,2,1,0:T(8,128)(2,1)S(1)}, bf16[1,16,32,256]{3,2,1,0:T(8,128)(2,1)}, u32[]{:S(2)}) copy-start(bf16[1,16,32,256]{3,2,1,0:T(8,128)(2,1)} %param.9) | copy-start | bytes 786436
  29.3 13.0 %copy-start.2 = (bf16[3,3,256,256]{3,2,1,0:T(8,128)(2,1)S(1)}, bf16[3,3,256,256]{3,2,1,0:T(8,128)(2,1)}, u32[]{:S(2)}) copy-start(bf16[3,3,256,256]{3,2,1,0:T(8,128)(2,1)} %param.8) | copy-start | bytes 3538948
  30.4 5.9 %collective-permute-start.4 = (bf16[1,32,256]{2,1,0:T(8,128)(2,1)S(1)}, bf16[1,32,256]{2,1,0:T(8,128)(2,1)S(1)}, u32[]{:S(2)}, u32[]{:S(2)}) collective-permute-start(bf16[1,32,256]{2,1,0:T(8,128)(2,1)S(1)} %get-tuple-element.49), channel_id=1, source_target_pairs={{0,4},{4,8},{8,12},{1,5},{5,9},{9,13},{2,6},{6,10},{10,14},{3,7},{... | collective-permute-start | bytes 49160 | tf_op jit(solution)/shard_map/ppermute | solution.py:14
  33.4 4.0 %collective-permute-start.5 = (bf16[1,32,256]{2,1,0:T(8,128)(2,1)S(1)}, bf16[1,32,256]{2,1,0:T(8,128)(2,1)S(1)}, u32[]{:S(2)}, u32[]{:S(2)}) collective-permute-start(bf16[1,32,256]{2,1,0:T(8,128)(2,1)S(1)} %get-tuple-element.50), channel_id=1, source_target_pairs={{4,0},{8,4},{12,8},{5,1},{9,5},{13,9},{6,2},{10,6},{14,10},{7,3},{... | collective-permute-start | bytes 49160 | tf_op jit(solution)/shard_map/ppermute | solution.py:15
  34.7 14.0 %collective-permute-start.9 = (bf16[16,32,256]{2,1,0:T(8,128)(2,1)S(1)}, bf16[16,32,256]{2,1,0:T(8,128)(2,1)S(1)}, u32[]{:S(2)}, u32[]{:S(2)}) collective-permute-start(bf16[16,32,256]{2,1,0:T(8,128)(2,1)S(1)} %bitcast.331), channel_id=1, source_target_pairs={{0,16},{16,0},{1,17},{17,1},{2,18},{18,2},{3,19},{19,3},{4,20},{20... | collective-permute-start | bytes 786440 | tf_op jit(solution)/shard_map/ppermute | solution.py:27
  37.5 5.1 %collective-permute-start.6 = (bf16[18,1,256]{2,1,0:T(2,128)(2,1)S(1)}, bf16[18,1,256]{2,1,0:T(2,128)(2,1)S(1)}, u32[]{:S(2)}, u32[]{:S(2)}) collective-permute-start(bf16[18,1,256]{2,1,0:T(2,128)(2,1)S(1)} %get-tuple-element.41), channel_id=1, source_target_pairs={{0,1},{1,2},{2,3},{4,5},{5,6},{6,7},{8,9},{9,10},{10,11},{12,13},{... | collective-permute-start | bytes 27656 | tf_op jit(solution)/shard_map/ppermute | solution.py:14
  40.9 5.7 %collective-permute-start.7 = (bf16[18,1,256]{2,1,0:T(2,128)(2,1)S(1)}, bf16[18,1,256]{2,1,0:T(2,128)(2,1)S(1)}, u32[]{:S(2)}, u32[]{:S(2)}) collective-permute-start(bf16[18,1,256]{2,1,0:T(2,128)(2,1)S(1)} %get-tuple-element.42), channel_id=1, source_target_pairs={{1,0},{2,1},{3,2},{5,4},{6,5},{7,6},{9,8},{10,9},{11,10},{13,12},{... | collective-permute-start | bytes 27656 | tf_op jit(solution)/shard_map/ppermute | solution.py:15
  49.4 6.8 %collective-permute-start.10 = (bf16[1,32,256]{2,1,0:T(8,128)(2,1)S(1)}, bf16[1,32,256]{2,1,0:T(8,128)(2,1)S(1)}, u32[]{:S(2)}, u32[]{:S(2)}) collective-permute-start(bf16[1,32,256]{2,1,0:T(8,128)(2,1)S(1)} %get-tuple-element.45), channel_id=1, source_target_pairs={{0,4},{4,8},{8,12},{1,5},{5,9},{9,13},{2,6},{6,10},{10,14},{3,7},{... | collective-permute-start | bytes 49160 | tf_op jit(solution)/shard_map/ppermute | solution.py:14
  52.6 3.9 %collective-permute-start.11 = (bf16[1,32,256]{2,1,0:T(8,128)(2,1)S(1)}, bf16[1,32,256]{2,1,0:T(8,128)(2,1)S(1)}, u32[]{:S(2)}, u32[]{:S(2)}) collective-permute-start(bf16[1,32,256]{2,1,0:T(8,128)(2,1)S(1)} %get-tuple-element.46), channel_id=1, source_target_pairs={{4,0},{8,4},{12,8},{5,1},{9,5},{13,9},{6,2},{10,6},{14,10},{7,3},{... | collective-permute-start | bytes 49160 | tf_op jit(solution)/shard_map/ppermute | solution.py:15
  56.1 7.9 %copy-start.3 = (f32[9,256,256]{2,1,0:T(8,128)}, f32[9,256,256]{2,1,0:T(8,128)S(1)}, u32[]{:S(2)}) copy-start(f32[9,256,256]{2,1,0:T(8,128)S(1)} %fusion.4) | copy-start | bytes 7077892
  56.5 6.3 %collective-permute-start.12 = (bf16[18,1,256]{2,1,0:T(2,128)(2,1)S(1)}, bf16[18,1,256]{2,1,0:T(2,128)(2,1)S(1)}, u32[]{:S(2)}, u32[]{:S(2)}) collective-permute-start(bf16[18,1,256]{2,1,0:T(2,128)(2,1)S(1)} %get-tuple-element.37), channel_id=1, source_target_pairs={{1,0},{2,1},{3,2},{5,4},{6,5},{7,6},{9,8},{10,9},{11,10},{13,12},{... | collective-permute-start | bytes 27656 | tf_op jit(solution)/shard_map/ppermute | solution.py:15
  57.8 6.0 %collective-permute-start.13 = (bf16[18,1,256]{2,1,0:T(2,128)(2,1)S(1)}, bf16[18,1,256]{2,1,0:T(2,128)(2,1)S(1)}, u32[]{:S(2)}, u32[]{:S(2)}) collective-permute-start(bf16[18,1,256]{2,1,0:T(2,128)(2,1)S(1)} %get-tuple-element.38), channel_id=1, source_target_pairs={{0,1},{1,2},{2,3},{4,5},{5,6},{6,7},{8,9},{9,10},{10,11},{12,13},{... | collective-permute-start | bytes 27656 | tf_op jit(solution)/shard_map/ppermute | solution.py:14
  71.6 0.8 copy-start.4
  72.5 8.9 %collective-permute-start.8 = (bf16[16,32,256]{2,1,0:T(8,128)(2,1)S(1)}, bf16[16,32,256]{2,1,0:T(8,128)(2,1)S(1)}, u32[]{:S(2)}, u32[]{:S(2)}) collective-permute-start(bf16[16,32,256]{2,1,0:T(8,128)(2,1)S(1)} %bitcast.332), channel_id=1, source_target_pairs={{0,16},{16,0},{1,17},{17,1},{2,18},{18,2},{3,19},{19,3},{4,20},{20... | collective-permute-start | bytes 786440 | tf_op jit(solution)/shard_map/ppermute | solution.py:27
  214.0 2.6 %copy-start.6 = (f32[128,256]{1,0:T(8,128)S(1)}, f32[128,256]{1,0:T(8,128)}, u32[]{:S(2)}) copy-start(f32[128,256]{1,0:T(8,128)} %get-tuple-element.62) | copy-start | bytes 393220
Sparse Core Ops, SparseCore 0:
  72.6 141.4 all-reduce.2
where the time goes:
time: 228 us; the launch traced here: 227 us
  waiting for transfers between devices  153 us (67%)
  starting transfers between devices  31.2 us (14%)
  between operations  14.7 us (6%)
  matrix products  14.2 us (6%)
  local copies, waits for them, and re-layouts  9.64 us (4%)
  other arithmetic  4.38 us (2%)
    psum x1, waiting for transfers between devices, per_device(): lax.psum((grad_first, grad_projection, grad_second), ('section', 'gy', 'g...  133 us
    ppermute x6, starting transfers between devices, padded_2(): before = lax.ppermute(last, axis, up)  20.3 us
    ppermute x6, waiting for transfers between devices, padded_2(): after = lax.ppermute(initial, axis, down)  12.2 us
    ppermute x6, starting transfers between devices, padded_2(): after = lax.ppermute(initial, axis, down)  7.88 us
    ppermute x2, waiting for transfers between devices, from_partner(): return lax.ppermute(block, axis, route)  7.47 us
    unnamed x20, local copies, waits for them, and re-layouts  7.35 us
    dot_general x18, matrix products, conv_slopes(): jnp.einsum('pc,pd->cd', piece, slope, preferred_element_type=jnp.float32)  5.6 us
    dot_general x18, matrix products, conv_forward(): jnp.dot(piece, kernel[row_tap, col_tap], preferred_element_type=jnp.float32)  4.91 us
  transfers between devices with their start and end apart: 15, of which 8 were waited for; matrix products, arithmetic and copies ran while one was open for 3% of the time, Pallas kernels for 0%

commit v1 on v0

--- a/solution.py
+++ b/solution.py
@@ -2,6 +2,11 @@
 import jax.numpy as jnp
 from jax import lax
 from jax.sharding import PartitionSpec as P
+from jax.lax import psum
+
+
+def _find_area(buf, chip_axis, shard_axis):
+    return psum(psum(buf, chip_axis), shard_axis)
 
 
 def padded_2(array, sides, width):
@@ -136,8 +141,8 @@
     grad_projection, pooled_slope = projection_back(pooled, back, projection)
     output = from_partner(output, "section", 0)
     grad_first = first_back(padded, before, pooled_slope)
-    grad_first, grad_projection, grad_second = lax.psum(
-        (grad_first, grad_projection, grad_second), ("section", "gy", "gx")
+    grad_first, grad_projection, grad_second = _find_area(
+        (grad_first, grad_projection, grad_second), "section", ("gy", "gx")
     )
     return (output[None], grad_first, grad_projection, grad_second)
 

time: 228 us -> 282 us (1.24)
  waiting for transfers between devices: 153 us -> 208 us
    psum x1 -> x2, waiting for transfers between devices: 133 us -> 187 us  [_find_area(): return psum(psum(buf, chip_axis), shard_axis)]
  transfers between devices with their start and end apart: 15 -> 16, of which waited for: 8 -> 9; matrix products, arithmetic and copies ran while one was open for 3% -> 2% of each run, Pallas kernels for 0% -> 0%
where the time goes in v1:
time: 282 us; the launch traced here: 281 us
  waiting for transfers between devices  208 us (74%)
  starting transfers between devices  30.2 us (11%)
  between operations  14.7 us (5%)
  matrix products  14.2 us (5%)
  local copies, waits for them, and re-layouts  9.64 us (3%)
  other arithmetic  4.4 us (2%)
    psum x2, waiting for transfers between devices, _find_area(): return psum(psum(buf, chip_axis), shard_axis)  187 us
    ppermute x6, starting transfers between devices, padded_2(): before = lax.ppermute(last, axis, up)  20.3 us
    ppermute x6, waiting for transfers between devices, padded_2(): after = lax.ppermute(initial, axis, down)  12.2 us
    ppermute x6, starting transfers between devices, padded_2(): after = lax.ppermute(initial, axis, down)  7.88 us
    ppermute x2, waiting for transfers between devices, from_partner(): return lax.ppermute(block, axis, route)  7.53 us
    unnamed x20, local copies, waits for them, and re-layouts  7.35 us
  transfers between devices with their start and end apart: 16, of which 9 were waited for; matrix products, arithmetic and copies ran while one was open for 2% of the time, Pallas kernels for 0%

profile of v1, /device:TPU:0, one launch (start us, length us, event | category | flops | bytes accessed | tf_op | source)
XLA Modules:
  0.0 281.3 jit_solution(14978144099598910813)
XLA Ops:
  7.2 0.8 slice_bitcast_fusion.5
  8.0 2.4 collective-permute-start
  10.4 1.3 collective-permute-start.1
  11.7 3.9 %collective-permute-done.1 = bf16[1,64,128]{2,1,0:T(8,128)(2,1)S(1)} collective-permute-done((bf16[1,64,128]{2,1,0:T(8,128)(2,1)S(1)}, bf16[1,64,128]{2,1,0:T(8,128)(2,1)S(1)}, u32[]{:S(2)}, u32[]{:S(2)}) %collective-permute-start.1) | collective-permute-done | bytes 16416 | tf_op jit(solution)/shard_map/ppermute | solution.py:20
  15.6 0.9 pad_maximum_fusion.17
  16.5 3.5 %collective-permute-start.2 = (bf16[34,1,128]{2,1,0:T(2,128)(2,1)S(1)}, bf16[34,1,128]{2,1,0:T(2,128)(2,1)S(1)}, u32[]{:S(2)}, u32[]{:S(2)}) collective-permute-start(bf16[34,1,128]{2,1,0:T(2,128)(2,1)S(1)} %get-tuple-element.18), channel_id=1, source_target_pairs={{0,1},{1,2},{2,3},{4,5},{5,6},{6,7},{8,9},{9,10},{10,11},{12,13},{... | collective-permute-start | bytes 26120 | tf_op jit(solution)/shard_map/ppermute | solution.py:19
  20.0 1.4 collective-permute-start.3
  21.5 1.3 pad_maximum_fusion.1
  23.1 2.7 collective-permute-done.3
  25.8 0.3 maximum_maximum_fusion
  26.2 0.6 fusion.85
  28.8 0.5 multiply_convert_fusion.1
  29.3 0.9 convert_reduce_fusion
  30.4 3.0 %collective-permute-start.4 = (bf16[1,32,256]{2,1,0:T(8,128)(2,1)S(1)}, bf16[1,32,256]{2,1,0:T(8,128)(2,1)S(1)}, u32[]{:S(2)}, u32[]{:S(2)}) collective-permute-start(bf16[1,32,256]{2,1,0:T(8,128)(2,1)S(1)} %get-tuple-element.52), channel_id=1, source_target_pairs={{0,4},{4,8},{8,12},{1,5},{5,9},{9,13},{2,6},{6,10},{10,14},{3,7},{... | collective-permute-start | bytes 49160 | tf_op jit(solution)/shard_map/ppermute | solution.py:19
  33.4 1.3 collective-permute-start.5
  34.7 1.6 collective-permute-start.9
  36.3 1.2 collective-permute-done.5
  37.5 3.5 %collective-permute-start.6 = (bf16[18,1,256]{2,1,0:T(2,128)(2,1)S(1)}, bf16[18,1,256]{2,1,0:T(2,128)(2,1)S(1)}, u32[]{:S(2)}, u32[]{:S(2)}) collective-permute-start(bf16[18,1,256]{2,1,0:T(2,128)(2,1)S(1)} %get-tuple-element.44), channel_id=1, source_target_pairs={{0,1},{1,2},{2,3},{4,5},{5,6},{6,7},{8,9},{9,10},{10,11},{12,13},{... | collective-permute-start | bytes 27656 | tf_op jit(solution)/shard_map/ppermute | solution.py:19
  40.9 1.3 collective-permute-start.7
  42.5 4.1 %collective-permute-done.7 = bf16[18,1,256]{2,1,0:T(2,128)(2,1)S(1)} collective-permute-done((bf16[18,1,256]{2,1,0:T(2,128)(2,1)S(1)}, bf16[18,1,256]{2,1,0:T(2,128)(2,1)S(1)}, u32[]{:S(2)}, u32[]{:S(2)}) %collective-permute-start.7) | collective-permute-done | bytes 9248 | tf_op jit(solution)/shard_map/ppermute | solution.py:20
  48.7 0.4 fusion.24
  49.4 3.2 %collective-permute-start.10 = (bf16[1,32,256]{2,1,0:T(8,128)(2,1)S(1)}, bf16[1,32,256]{2,1,0:T(8,128)(2,1)S(1)}, u32[]{:S(2)}, u32[]{:S(2)}) collective-permute-start(bf16[1,32,256]{2,1,0:T(8,128)(2,1)S(1)} %get-tuple-element.48), channel_id=1, source_target_pairs={{0,4},{4,8},{8,12},{1,5},{5,9},{9,13},{2,6},{6,10},{10,14},{3,7},{... | collective-permute-start | bytes 49160 | tf_op jit(solution)/shard_map/ppermute | solution.py:19
  52.6 1.3 collective-permute-start.11
  56.2 0.3 collective-permute-done.11
  56.5 1.3 collective-permute-start.12
  57.8 4.7 %collective-permute-start.13 = (bf16[18,1,256]{2,1,0:T(2,128)(2,1)S(1)}, bf16[18,1,256]{2,1,0:T(2,128)(2,1)S(1)}, u32[]{:S(2)}, u32[]{:S(2)}) collective-permute-start(bf16[18,1,256]{2,1,0:T(2,128)(2,1)S(1)} %get-tuple-element.41), channel_id=1, source_target_pairs={{0,1},{1,2},{2,3},{4,5},{5,6},{6,7},{8,9},{9,10},{10,11},{12,13},{... | collective-permute-start | bytes 27656 | tf_op jit(solution)/shard_map/ppermute | solution.py:19
  62.9 0.9 collective-permute-done.13
  66.4 0.9 fusion.91
  67.5 0.5 broadcast_in_dim.10
  68.0 0.4 multiply_convert_fusion
  68.4 0.3 fusion.23
  68.8 0.4 fusion.22
  69.1 0.4 fusion.21
  69.5 0.4 fusion.20
  69.8 0.4 fusion.19
  70.2 0.4 fusion.18
  70.5 0.4 fusion.17
  70.9 0.4 fusion.16
  71.3 0.4 fusion.15
  71.6 0.8 copy-done.4
  72.5 87.1 %all-reduce.7.cloned.1.call-done = (f32[3,3,128,128]{3,2,1,0:T(8,128)}, f32[128,256]{1,0:T(8,128)}, f32[3,3,256,256]{3,2,1,0:T(8,128)}) async-done(((f32[3,3,128,128]{3,2,1,0:T(8,128)}, f32[128,256]{1,0:T(8,128)}, f32[3,3,256,256]{3,2,1,0:T(8,128)}), (f32[3,3,128,128]{3,2,1,0:T(8,128)}, f32[128,256]{1,0:T(8,128)}, f32[3,3,256,256]{3,2,1,0:T(8,128)})) %all-reduce.7.cloned.1.call-update) | async-done | bytes 3080208 | tf_op jit(solution)/shard_map/psum | solution.py:9
  159.7 0.4 collective-permute-start.8
  160.1 7.5 %collective-permute-done.8 = bf16[16,32,256]{2,1,0:T(8,128)(2,1)S(1)} collective-permute-done((bf16[16,32,256]{2,1,0:T(8,128)(2,1)S(1)}, bf16[16,32,256]{2,1,0:T(8,128)(2,1)S(1)}, u32[]{:S(2)}, u32[]{:S(2)}) %collective-permute-start.8) | collective-permute-done | bytes 262176 | tf_op jit(solution)/shard_map/ppermute | solution.py:32
  167.6 100.3 %all-reduce.5.cloned.1.call-done = (f32[3,3,128,128]{3,2,1,0:T(8,128)}, f32[128,256]{1,0:T(8,128)}, f32[3,3,256,256]{3,2,1,0:T(8,128)}) async-done(((f32[3,3,128,128]{3,2,1,0:T(8,128)}, f32[128,256]{1,0:T(8,128)}, f32[3,3,256,256]{3,2,1,0:T(8,128)}), (f32[3,3,128,128]{3,2,1,0:T(8,128)}, f32[128,256]{1,0:T(8,128)}, f32[3,3,256,256]{3,2,1,0:T(8,128)})) %all-reduce.5.cloned.1.call-update) | async-done | bytes 3080208 | tf_op jit(solution)/shard_map/psum | solution.py:9
  267.9 0.7 copy.34
  268.6 1.9 copy.35
  270.6 0.7 copy.36
  271.2 3.2 %copy.37 = f32[3,3,256,256]{3,2,1,0:T(8,128)} copy(f32[3,3,256,256]{3,2,1,0:T(8,128)} %get-tuple-element.66) | data formatting | bytes 4718592
  (75 shorter events, 10.4 us)
Async XLA Ops:
  7.2 23.0 %copy-start = (bf16[128,256]{1,0:T(8,128)(2,1)S(1)}, bf16[128,256]{1,0:T(8,128)(2,1)}, u32[]{:S(2)}) copy-start(bf16[128,256]{1,0:T(8,128)(2,1)} %param.7) | copy-start | bytes 196612
  7.2 15.6 %copy-start.5 = (bf16[3,3,128,128]{3,2,1,0:T(8,128)(2,1)S(1)}, bf16[3,3,128,128]{3,2,1,0:T(8,128)(2,1)}, u32[]{:S(2)}) copy-start(bf16[3,3,128,128]{3,2,1,0:T(8,128)(2,1)} %param.6) | copy-start | bytes 884740
  7.2 152.4 %all-reduce.7.cloned.1.call-start = ((), (), s32[]{:S(2)}) async-start(), calls=%async_computation.1 | async-start | bytes 6160384 | tf_op jit(solution)/shard_map/psum | solution.py:9
  8.0 3.7 %collective-permute-start = (bf16[1,64,128]{2,1,0:T(8,128)(2,1)S(1)}, bf16[1,64,128]{2,1,0:T(8,128)(2,1)S(1)}, u32[]{:S(2)}, u32[]{:S(2)}) collective-permute-start(bf16[1,64,128]{2,1,0:T(8,128)(2,1)S(1)} %get-tuple-element.24), channel_id=1, source_target_pairs={{0,4},{4,8},{8,12},{1,5},{5,9},{9,13},{2,6},{6,10},{10,14},{3,7},{... | collective-permute-start | bytes 49160 | tf_op jit(solution)/shard_map/ppermute | solution.py:19
  10.4 5.2 %collective-permute-start.1 = (bf16[1,64,128]{2,1,0:T(8,128)(2,1)S(1)}, bf16[1,64,128]{2,1,0:T(8,128)(2,1)S(1)}, u32[]{:S(2)}, u32[]{:S(2)}) collective-permute-start(bf16[1,64,128]{2,1,0:T(8,128)(2,1)S(1)} %get-tuple-element.25), channel_id=1, source_target_pairs={{4,0},{8,4},{12,8},{5,1},{9,5},{13,9},{6,2},{10,6},{14,10},{7,3},{... | collective-permute-start | bytes 49160 | tf_op jit(solution)/shard_map/ppermute | solution.py:20
  16.5 6.5 %collective-permute-start.2 = (bf16[34,1,128]{2,1,0:T(2,128)(2,1)S(1)}, bf16[34,1,128]{2,1,0:T(2,128)(2,1)S(1)}, u32[]{:S(2)}, u32[]{:S(2)}) collective-permute-start(bf16[34,1,128]{2,1,0:T(2,128)(2,1)S(1)} %get-tuple-element.18), channel_id=1, source_target_pairs={{0,1},{1,2},{2,3},{4,5},{5,6},{6,7},{8,9},{9,10},{10,11},{12,13},{... | collective-permute-start | bytes 26120 | tf_op jit(solution)/shard_map/ppermute | solution.py:19
  20.0 5.8 %copy-start.1 = (bf16[1,32,64,128]{3,2,1,0:T(8,128)(2,1)S(1)}, bf16[1,32,64,128]{3,2,1,0:T(8,128)(2,1)}, u32[]{:S(2)}) copy-start(bf16[1,32,64,128]{3,2,1,0:T(8,128)(2,1)} %param.5) | copy-start | bytes 1572868
  20.0 5.8 %collective-permute-start.3 = (bf16[34,1,128]{2,1,0:T(2,128)(2,1)S(1)}, bf16[34,1,128]{2,1,0:T(2,128)(2,1)S(1)}, u32[]{:S(2)}, u32[]{:S(2)}) collective-permute-start(bf16[34,1,128]{2,1,0:T(2,128)(2,1)S(1)} %get-tuple-element.19), channel_id=1, source_target_pairs={{1,0},{2,1},{3,2},{5,4},{6,5},{7,6},{9,8},{10,9},{11,10},{13,12},{... | collective-permute-start | bytes 26120 | tf_op jit(solution)/shard_map/ppermute | solution.py:20
  29.2 5.4 %copy-start.7 = (bf16[1,16,32,256]{3,2,1,0:T(8,128)(2,1)S(1)}, bf16[1,16,32,256]{3,2,1,0:T(8,128)(2,1)}, u32[]{:S(2)}) copy-start(bf16[1,16,32,256]{3,2,1,0:T(8,128)(2,1)} %param.9) | copy-start | bytes 786436
  29.3 13.0 %copy-start.2 = (bf16[3,3,256,256]{3,2,1,0:T(8,128)(2,1)S(1)}, bf16[3,3,256,256]{3,2,1,0:T(8,128)(2,1)}, u32[]{:S(2)}) copy-start(bf16[3,3,256,256]{3,2,1,0:T(8,128)(2,1)} %param.8) | copy-start | bytes 3538948
  30.4 5.9 %collective-permute-start.4 = (bf16[1,32,256]{2,1,0:T(8,128)(2,1)S(1)}, bf16[1,32,256]{2,1,0:T(8,128)(2,1)S(1)}, u32[]{:S(2)}, u32[]{:S(2)}) collective-permute-start(bf16[1,32,256]{2,1,0:T(8,128)(2,1)S(1)} %get-tuple-element.52), channel_id=1, source_target_pairs={{0,4},{4,8},{8,12},{1,5},{5,9},{9,13},{2,6},{6,10},{10,14},{3,7},{... | collective-permute-start | bytes 49160 | tf_op jit(solution)/shard_map/ppermute | solution.py:19
  33.4 4.0 %collective-permute-start.5 = (bf16[1,32,256]{2,1,0:T(8,128)(2,1)S(1)}, bf16[1,32,256]{2,1,0:T(8,128)(2,1)S(1)}, u32[]{:S(2)}, u32[]{:S(2)}) collective-permute-start(bf16[1,32,256]{2,1,0:T(8,128)(2,1)S(1)} %get-tuple-element.53), channel_id=1, source_target_pairs={{4,0},{8,4},{12,8},{5,1},{9,5},{13,9},{6,2},{10,6},{14,10},{7,3},{... | collective-permute-start | bytes 49160 | tf_op jit(solution)/shard_map/ppermute | solution.py:20
  34.7 14.0 %collective-permute-start.9 = (bf16[16,32,256]{2,1,0:T(8,128)(2,1)S(1)}, bf16[16,32,256]{2,1,0:T(8,128)(2,1)S(1)}, u32[]{:S(2)}, u32[]{:S(2)}) collective-permute-start(bf16[16,32,256]{2,1,0:T(8,128)(2,1)S(1)} %bitcast.331), channel_id=1, source_target_pairs={{0,16},{16,0},{1,17},{17,1},{2,18},{18,2},{3,19},{19,3},{4,20},{20... | collective-permute-start | bytes 786440 | tf_op jit(solution)/shard_map/ppermute | solution.py:32
  37.5 5.1 %collective-permute-start.6 = (bf16[18,1,256]{2,1,0:T(2,128)(2,1)S(1)}, bf16[18,1,256]{2,1,0:T(2,128)(2,1)S(1)}, u32[]{:S(2)}, u32[]{:S(2)}) collective-permute-start(bf16[18,1,256]{2,1,0:T(2,128)(2,1)S(1)} %get-tuple-element.44), channel_id=1, source_target_pairs={{0,1},{1,2},{2,3},{4,5},{5,6},{6,7},{8,9},{9,10},{10,11},{12,13},{... | collective-permute-start | bytes 27656 | tf_op jit(solution)/shard_map/ppermute | solution.py:19
  40.9 5.7 %collective-permute-start.7 = (bf16[18,1,256]{2,1,0:T(2,128)(2,1)S(1)}, bf16[18,1,256]{2,1,0:T(2,128)(2,1)S(1)}, u32[]{:S(2)}, u32[]{:S(2)}) collective-permute-start(bf16[18,1,256]{2,1,0:T(2,128)(2,1)S(1)} %get-tuple-element.45), channel_id=1, source_target_pairs={{1,0},{2,1},{3,2},{5,4},{6,5},{7,6},{9,8},{10,9},{11,10},{13,12},{... | collective-permute-start | bytes 27656 | tf_op jit(solution)/shard_map/ppermute | solution.py:20
  49.4 6.8 %collective-permute-start.10 = (bf16[1,32,256]{2,1,0:T(8,128)(2,1)S(1)}, bf16[1,32,256]{2,1,0:T(8,128)(2,1)S(1)}, u32[]{:S(2)}, u32[]{:S(2)}) collective-permute-start(bf16[1,32,256]{2,1,0:T(8,128)(2,1)S(1)} %get-tuple-element.48), channel_id=1, source_target_pairs={{0,4},{4,8},{8,12},{1,5},{5,9},{9,13},{2,6},{6,10},{10,14},{3,7},{... | collective-permute-start | bytes 49160 | tf_op jit(solution)/shard_map/ppermute | solution.py:19
  52.6 3.9 %collective-permute-start.11 = (bf16[1,32,256]{2,1,0:T(8,128)(2,1)S(1)}, bf16[1,32,256]{2,1,0:T(8,128)(2,1)S(1)}, u32[]{:S(2)}, u32[]{:S(2)}) collective-permute-start(bf16[1,32,256]{2,1,0:T(8,128)(2,1)S(1)} %get-tuple-element.49), channel_id=1, source_target_pairs={{4,0},{8,4},{12,8},{5,1},{9,5},{13,9},{6,2},{10,6},{14,10},{7,3},{... | collective-permute-start | bytes 49160 | tf_op jit(solution)/shard_map/ppermute | solution.py:20
  56.1 7.9 %copy-start.3 = (f32[9,256,256]{2,1,0:T(8,128)}, f32[9,256,256]{2,1,0:T(8,128)S(1)}, u32[]{:S(2)}) copy-start(f32[9,256,256]{2,1,0:T(8,128)S(1)} %fusion.4) | copy-start | bytes 7077892
  56.5 6.3 %collective-permute-start.12 = (bf16[18,1,256]{2,1,0:T(2,128)(2,1)S(1)}, bf16[18,1,256]{2,1,0:T(2,128)(2,1)S(1)}, u32[]{:S(2)}, u32[]{:S(2)}) collective-permute-start(bf16[18,1,256]{2,1,0:T(2,128)(2,1)S(1)} %get-tuple-element.40), channel_id=1, source_target_pairs={{1,0},{2,1},{3,2},{5,4},{6,5},{7,6},{9,8},{10,9},{11,10},{13,12},{... | collective-permute-start | bytes 27656 | tf_op jit(solution)/shard_map/ppermute | solution.py:20
  57.8 6.0 %collective-permute-start.13 = (bf16[18,1,256]{2,1,0:T(2,128)(2,1)S(1)}, bf16[18,1,256]{2,1,0:T(2,128)(2,1)S(1)}, u32[]{:S(2)}, u32[]{:S(2)}) collective-permute-start(bf16[18,1,256]{2,1,0:T(2,128)(2,1)S(1)} %get-tuple-element.41), channel_id=1, source_target_pairs={{0,1},{1,2},{2,3},{4,5},{5,6},{6,7},{8,9},{9,10},{10,11},{12,13},{... | collective-permute-start | bytes 27656 | tf_op jit(solution)/shard_map/ppermute | solution.py:19
  71.6 0.8 copy-start.4
  72.5 195.5 %all-reduce.5.cloned.1.call-start = ((), (), s32[]{:S(2)}) async-start(), calls=%async_computation | async-start | bytes 6160384 | tf_op jit(solution)/shard_map/psum | solution.py:9
  159.7 7.9 %collective-permute-start.8 = (bf16[16,32,256]{2,1,0:T(8,128)(2,1)S(1)}, bf16[16,32,256]{2,1,0:T(8,128)(2,1)S(1)}, u32[]{:S(2)}, u32[]{:S(2)}) collective-permute-start(bf16[16,32,256]{2,1,0:T(8,128)(2,1)S(1)} %bitcast.332), channel_id=1, source_target_pairs={{0,16},{16,0},{1,17},{17,1},{2,18},{18,2},{3,19},{19,3},{4,20},{20... | collective-permute-start | bytes 786440 | tf_op jit(solution)/shard_map/ppermute | solution.py:32
  267.9 2.6 copy-start.6
Sparse Core Ops, SparseCore 0:
  72.6 86.9 all-reduce.6
  163.5 104.3 all-reduce.4
